TPU v7x, 32 devices: a whole 2x2x4 slice. The times are simulated.
32 devices in a mesh: row: 8 (over z, y), col: 4 (over x, core).
Axes of the slice: x: 2, y: 2, z: 4, core: 2. Of those that a mesh axis runs over, the one named last changes fastest.
Arguments:
- trailing: bfloat16 [12288, 12288], P('row', 'col'), may hold values from -6 to 6
- rows_a: int32 [8, 12], replicated, may hold values from 0 to 11, as said below
- counts_a: int32 [8], replicated, may hold values from 1 to 12, as said below
- factor_a: bfloat16 [12288, 512], P('row'), may hold values from -0.0546875 to 0.0546875
- rows_b: int32 [8, 12], replicated, may hold values from 0 to 11, as said below
- counts_b: int32 [8], replicated, may hold values from 1 to 12, as said below
- factor_b: bfloat16 [12288, 512], P('row'), may hold values from -0.0546875 to 0.0546875
- factor_top: bfloat16 [512, 512], replicated, may hold values from -0.25 to 0.25
- base_a: float32 [512, 512], P('col'), may hold values from -3 to 3
- base_b: float32 [512, 512], P('col'), may hold values from -3 to 3
Outputs:
- column_a: bfloat16 [12288, 512], P('row')
- diag_a: float32 [512, 512], P('col')
- column_b: bfloat16 [12288, 512], P('row')
- top_b: bfloat16 [512, 512], P('col')
- diag_b: float32 [512, 512], P('col')
Inputs may be any that keep to these rules, and one draw needn't show every extreme that they name: `rows_a`: the first counts_a[r] entries of row r are distinct; the rest of the row is padding. `counts_a`: some owner uses all 12 slots in every draw. `rows_b`: the first counts_b[r] entries of row r are distinct and lie among the first counts_a[r] entries of row r of rows_a; the rest is padding. counts_b[r] <= counts_a[r]; some owner uses all 12 slots in every draw.
All inputs are finite; a program needn't handle non-finite values.
Results may differ from a plain program's by a relative error of at most 0.007.
Values may be sent and summed in bfloat16 or wider, within the bound.
A program may use at most 128 MiB of HBM per device.

v0:
```python
import jax
import jax.numpy as jnp
from jax import lax
from jax.sharding import PartitionSpec as P

BS = 128
W = 512
RBD = 12
PAD = 12


def spread_2(value, axis, source):
    kept = jnp.where(lax.axis_index(axis) == source, value, 0).astype(value.dtype)
    return lax.psum(kept, axis)


def contract_rows(former, latter):
    return lax.dot_general(
        former, latter, (((0,), (0,)), ((), ())), preferred_element_type=jnp.float32
    )


def slot_live(counts, owner_idx):
    live_count = lax.dynamic_index_in_dim(counts, owner_idx, 0, keepdims=False)
    return jnp.arange(PAD, dtype=jnp.int32) < live_count


def on_device(
    trailing, rows_a, counts_a, factor_a, rows_b, counts_b, factor_b, factor_top, base_a, base_b
):
    row_count = lax.axis_size("row")
    col_count = lax.axis_size("col")
    fanout = row_count // col_count
    row_index = lax.axis_index("row")
    col_index = lax.axis_index("col")
    col_blocks = trailing.shape[1] // BS
    part_width = W // col_count
    slot_rows = PAD * BS
    share_rows = slot_rows // col_count
    width_start = col_index * part_width
    share_start = col_index * share_rows
    slab_blocks = trailing.reshape(RBD, BS, trailing.shape[1])

    def row_gate(live_rows):
        return jnp.repeat(live_rows.astype(jnp.float32), BS)[:, None]

    def partial_product(rows, counts, factor):
        own_rows = lax.dynamic_index_in_dim(rows, row_index, 0, keepdims=False)
        row_slab = jnp.take(slab_blocks, own_rows, axis=0).reshape(slot_rows, trailing.shape[1])
        pieces = []
        targets = []
        flags = []
        for offset in range(fanout):
            source = col_index + offset * col_count
            pieces.append(spread_2(factor, "row", source))
            src_rows = lax.dynamic_index_in_dim(rows, source, 0, keepdims=False)
            targets.append(src_rows * fanout + offset)
            flags.append(slot_live(counts, source))
        received = jnp.stack(pieces).reshape(fanout * PAD, BS * W)
        target = jnp.concatenate(targets)
        live_src = jnp.concatenate(flags)
        selector = (
            (jnp.arange(col_blocks, dtype=jnp.int32)[:, None] == target[None, :])
            & live_src[None, :]
        ).astype(jnp.bfloat16)
        spread = jnp.dot(selector, received, preferred_element_type=jnp.float32).astype(
            jnp.bfloat16
        )
        return jnp.dot(
            row_slab, spread.reshape(col_blocks * BS, W), preferred_element_type=jnp.float32
        )

    def finish(partial_value, live_rows, addend):
        gate = row_gate(live_rows)
        reduced = lax.psum_scatter(partial_value, "col", scatter_dimension=0, tiled=True)
        if addend is not None:
            reduced = reduced + addend(share_start, share_rows)
        share_gate = lax.dynamic_slice_in_dim(gate, share_start, share_rows, 0)
        share_out = (-reduced * share_gate).astype(jnp.bfloat16)
        return lax.all_gather(share_out, "col", axis=0, tiled=True)

    def row_sums(pieces_in):
        return lax.psum(pieces_in, "row")

    live_a = slot_live(counts_a, row_index)
    live_b = slot_live(counts_b, row_index)
    column_a = finish(partial_product(rows_a, counts_a, factor_a), live_a, None)
    own_rows_a = lax.dynamic_index_in_dim(rows_a, row_index, 0, keepdims=False)
    own_rows_b = lax.dynamic_index_in_dim(rows_b, row_index, 0, keepdims=False)
    pairing = (
        (own_rows_b[:, None] == own_rows_a[None, :]) & live_a[None, :] & live_b[:, None]
    ).astype(jnp.bfloat16)
    carried = (
        jnp.dot(pairing, column_a.reshape(PAD, BS * W), preferred_element_type=jnp.float32)
        .astype(jnp.bfloat16)
        .reshape(slot_rows, W)
    )
    width_a = lax.dynamic_slice_in_dim(column_a, width_start, part_width, 1)
    width_c = lax.dynamic_slice_in_dim(carried, width_start, part_width, 1)
    sums_a = row_sums((contract_rows(width_a, factor_a), contract_rows(width_c, factor_b)))
    diag_a = base_a - sums_a[0]
    top_b = (
        -(
            sums_a[1]
            + jnp.dot(diag_a, factor_top.astype(jnp.float32), precision=lax.Precision.HIGHEST)
        )
    ).astype(jnp.bfloat16)

    def cross_rows(first_row, row_total):
        picked = lax.dynamic_slice_in_dim(carried, first_row, row_total, 0)
        return jnp.dot(picked, factor_top, preferred_element_type=jnp.float32)

    column_b = finish(partial_product(rows_b, counts_b, factor_b), live_b, cross_rows)
    width_b = lax.dynamic_slice_in_dim(column_b, width_start, part_width, 1)
    sums_b = row_sums((contract_rows(width_b, factor_b),))
    top_whole = lax.all_gather(top_b, "col", axis=0, tiled=True)
    top_cols = lax.dynamic_slice_in_dim(top_whole, width_start, part_width, 1)
    diag_b = base_b - sums_b[0] - contract_rows(top_cols, factor_top)
    return (column_a, diag_a, column_b, top_b, diag_b)


def solution(mesh):
    in_specs = (
        P("row", "col"),
        P(),
        P(),
        P("row", None),
        P(),
        P(),
        P("row", None),
        P(),
        P("col", None),
        P("col", None),
    )
    out_specs = (P("row", None), P("col", None), P("row", None), P("col", None), P("col", None))
    return jax.shard_map(
        on_device, mesh=mesh, in_specs=in_specs, out_specs=out_specs, check_vma=False
    )
```

profile of v0, /device:TPU:0, one launch (start us, length us, event | category | flops | bytes accessed | tf_op | source)
XLA Modules:
  0.0 484.4 jit_solution(11630658327107411684)
XLA Ops:
  7.2 4.8 select_bitcast_fusion.1
  13.5 9.4 %gather_fusion = bf16[12,128,3072]{2,1,0:T(8,128)(2,1)} fusion(bf16[12,128,3072]{2,1,0:T(8,128)(2,1)} %bitcast.59, s32[1024]{0:T(1024)S(1)} %pad_clamp_fusion.1), kind=kCustom, calls=%fused_computation.clone | custom fusion | bytes 18874416 | tf_op jit(solution)/shard_map/jit(_take)/gather | solution.py:49
  26.7 8.4 %broadcast_select_fusion.1 = bf16[12,128,3072]{2,1,0:T(8,128)(2,1)} fusion(bf16[12,128,3072]{2,1,0:T(8,128)(2,1)} %gather_fusion, pred[12]{0:T(512)(128)(4,1)S(1)} %get-tuple-element.15), kind=kLoop, calls=%fused_computation.6 | loop fusion | flops 4718592 | bytes 18874380 | tf_op jit(solution)/shard_map/jit(_take)/select_n | solution.py:49
  35.0 191.1 %all-reduce.7.cloned.1.call-done = (bf16[1,1536,512]{2,1,0:T(8,128)(2,1)}, bf16[1,1536,512]{2,1,0:T(8,128)(2,1)}, bf16[1,1536,512]{2,1,0:T(8,128)(2,1)}, bf16[1,1536,512]{2,1,0:T(8,128)(2,1)}) async-done(((bf16[1,1536,512]{2,1,0:T(8,128)(2,1)}, bf16[1,1536,512]{2,1,0:T(8,128)(2,1)}, bf16[1,1536,512]{2,1,0:T(8,128)(2,1)}, bf16[1,1536,512]{2,1,0:T(8,128)(2,1)}), (bf16[1,1536,512]{2,1,0:T(8,128)(2,1)}, ...) | async-done | bytes 6291472 | tf_op jit(solution)/shard_map/psum | solution.py:14
  226.1 3.8 pad_maximum_fusion
  229.9 5.2 %reshape.70 = bf16[24,65536]{1,0:T(8,128)(2,1)} reshape(bf16[2,1536,512]{2,1,0:T(8,128)(2,1)} %pad_maximum_fusion) | data formatting | bytes 6291456 | tf_op jit(solution)/shard_map/reshape | solution.py:59
  235.1 4.5 convolution_convert_fusion.1
  239.6 5.2 %reshape.71 = bf16[3072,512]{1,0:T(8,128)(2,1)} reshape(bf16[24,65536]{1,0:T(8,128)(2,1)} %convolution_convert_fusion.1) | data formatting | bytes 6291456 | tf_op jit(solution)/shard_map/reshape | solution.py:70
  244.8 10.6 %fusion.53 = f32[1536,512]{1,0:T(8,128)} fusion(bf16[1536,3072]{1,0:T(8,128)(2,1)} %bitcast.62, bf16[3072,512]{1,0:T(8,128)(2,1)} %reshape.71), kind=kOutput, calls=%fused_computation.96 | convolution fusion | flops 4831838208 | bytes 15728640 | tf_op jit(solution)/shard_map/dot_general | solution.py:69
  255.5 9.7 %gather_fusion.1 = bf16[12,128,3072]{2,1,0:T(8,128)(2,1)} fusion(bf16[12,128,3072]{2,1,0:T(8,128)(2,1)} %bitcast.60, s32[1024]{0:T(1024)S(1)} %pad_clamp_fusion), kind=kCustom, calls=%fused_computation.1.clone | custom fusion | bytes 18874416 | tf_op jit(solution)/shard_map/jit(_take)/gather | solution.py:49
  267.3 8.4 %broadcast_select_fusion = bf16[12,128,3072]{2,1,0:T(8,128)(2,1)} fusion(bf16[12,128,3072]{2,1,0:T(8,128)(2,1)} %gather_fusion.1, pred[12]{0:T(512)(128)(4,1)S(1)} %get-tuple-element.13), kind=kLoop, calls=%fused_computation.5 | loop fusion | flops 4718592 | bytes 18874380 | tf_op jit(solution)/shard_map/jit(_take)/select_n | solution.py:49
  275.8 16.7 %reduce-scatter.3.cloned.1.call-done = f32[384,512]{1,0:T(8,128)} async-done(((f32[1536,512]{1,0:T(8,128)}), f32[384,512]{1,0:T(8,128)}) %reduce-scatter.3.cloned.1.call-update) | async-done | bytes 786448 | tf_op jit(solution)/shard_map/reduce_scatter | solution.py:75
  294.8 3.4 pad_maximum_fusion.1
  298.1 5.2 %reshape.73 = bf16[24,65536]{1,0:T(8,128)(2,1)} reshape(bf16[2,1536,512]{2,1,0:T(8,128)(2,1)} %pad_maximum_fusion.1) | data formatting | bytes 6291456 | tf_op jit(solution)/shard_map/reshape | solution.py:59
  303.3 4.5 convolution_convert_fusion
  307.9 5.2 %reshape.74 = bf16[3072,512]{1,0:T(8,128)(2,1)} reshape(bf16[24,65536]{1,0:T(8,128)(2,1)} %convolution_convert_fusion) | data formatting | bytes 6291456 | tf_op jit(solution)/shard_map/reshape | solution.py:70
  313.0 10.6 %fusion.54 = f32[1536,512]{1,0:T(8,128)} fusion(bf16[1536,3072]{1,0:T(8,128)(2,1)} %bitcast.61, bf16[3072,512]{1,0:T(8,128)(2,1)} %reshape.74), kind=kOutput, calls=%fused_computation.97 | convolution fusion | flops 4831838208 | bytes 15728640 | tf_op jit(solution)/shard_map/dot_general | solution.py:69
  330.1 3.6 reshape.76
  333.7 28.0 %reduce-scatter.5.cloned.1.call-done = f32[384,512]{1,0:T(8,128)} async-done(((f32[1536,512]{1,0:T(8,128)}), f32[384,512]{1,0:T(8,128)}) %reduce-scatter.5.cloned.1.call-update) | async-done | bytes 786448 | tf_op jit(solution)/shard_map/reduce_scatter | solution.py:75
  361.7 2.4 fusion.2
  366.3 2.7 fusion.10
  369.0 14.9 %all-gather.5.cloned.1.call-done = bf16[1536,512]{1,0:T(8,128)(2,1)} async-done(((bf16[384,512]{1,0:T(8,128)(2,1)}), bf16[1536,512]{1,0:T(8,128)(2,1)}) %all-gather.5.cloned.1.call-update) | async-done | bytes 1572880 | tf_op jit(solution)/shard_map/all_gather | solution.py:80
  386.1 77.7 %all-reduce.5.cloned.1.call-done = (f32[128,512]{1,0:T(8,128)}, f32[128,512]{1,0:T(8,128)}, f32[128,512]{1,0:T(8,128)}) async-done(((f32[128,512]{1,0:T(8,128)}, f32[128,512]{1,0:T(8,128)}, f32[128,512]{1,0:T(8,128)}), (f32[128,512]{1,0:T(8,128)}, f32[128,512]{1,0:T(8,128)}, f32[128,512]{1,0:T(8,128)})) %all-reduce.5.cloned.1.call-update) | async-done | bytes 786448 | tf_op jit(solution)/shard_map/psum | solution.py:83
  466.2 7.2 %all_gather.11 = bf16[512,512]{1,0:T(8,128)(2,1)S(1)} all-gather(bf16[128,512]{1,0:T(8,128)(2,1)S(1)} %fusion.4), channel_id=1, replica_groups=mesh['row'=8,'col'=4] {'col'}, dimensions={0}, use_global_device_ids=true | all-gather | bytes 655360 | tf_op jit(solution)/shard_map/all_gather | solution.py:116
  (70 shorter events, 27.0 us)
Async XLA Ops:
  7.2 354.6 %copy-start = (bf16[512,512]{1,0:T(8,128)(2,1)S(1)}, bf16[512,512]{1,0:T(8,128)(2,1)}, u32[]{:S(2)}) copy-start(bf16[512,512]{1,0:T(8,128)(2,1)} %param.19) | copy-start | bytes 1572868
  7.2 218.9 %all-reduce.7.cloned.1.call-start = ((), (), s32[]{:S(2)}) async-start(), calls=%async_computation.7 | async-start | bytes 12582912 | tf_op jit(solution)/shard_map/psum | solution.py:14
  12.0 280.5 %reduce-scatter.3.cloned.1.call-start = ((), (), s32[]{:S(2)}) async-start(), calls=%async_computation.2 | async-start | bytes 3932160 | tf_op jit(solution)/shard_map/reduce_scatter | solution.py:75
  13.5 9.5 %copy-start.9 = (s32[8]{0:T(128)S(1)}, s32[8]{0:T(128)}, u32[]{:S(2)}) copy-start(s32[8]{0:T(128)} %param.17) | copy-start | bytes 100
  13.5 9.4 %copy-start.10 = (s32[8]{0:T(128)S(1)}, s32[8]{0:T(128)}, u32[]{:S(2)}) copy-start(s32[8]{0:T(128)} %param.14) | copy-start | bytes 100
  255.4 70.4 %all-gather.3.cloned.1.call-start = ((), (), s32[]{:S(2)}) async-start(), calls=%async_computation.3 | async-start | bytes 1966080 | tf_op jit(solution)/shard_map/all_gather | solution.py:80
  267.3 27.5 %copy-start.4 = (bf16[1,1536,512]{2,1,0:T(8,128)(2,1)S(1)}, bf16[1,1536,512]{2,1,0:T(8,128)(2,1)}, u32[]{:S(2)}) copy-start(bf16[1,1536,512]{2,1,0:T(8,128)(2,1)} %get-tuple-element.11) | copy-start | bytes 4718596
  294.5 67.2 %reduce-scatter.5.cloned.1.call-start = ((), (), s32[]{:S(2)}) async-start(), calls=%async_computation.4 | async-start | bytes 3932160 | tf_op jit(solution)/shard_map/reduce_scatter | solution.py:75
  323.7 60.3 %all-gather.5.cloned.1.call-start = ((), (), s32[]{:S(2)}) async-start(), calls=%async_computation.5 | async-start | bytes 1966080 | tf_op jit(solution)/shard_map/all_gather | solution.py:80
  330.1 34.1 %copy-start.1 = (bf16[1536,512]{1,0:T(8,128)(2,1)S(1)}, bf16[1536,512]{1,0:T(8,128)(2,1)}, u32[]{:S(2)}) copy-start(bf16[1536,512]{1,0:T(8,128)(2,1)} %param.18) | copy-start | bytes 4718596
  364.1 99.6 %all-reduce.5.cloned.1.call-start = ((), (), s32[]{:S(2)}) async-start(), calls=%async_computation.6 | async-start | bytes 1572864 | tf_op jit(solution)/shard_map/psum | solution.py:83
  366.3 97.4 %copy-start.7 = (f32[128,512]{1,0:T(8,128)S(1)}, f32[128,512]{1,0:T(8,128)}, u32[]{:S(2)}) copy-start(f32[128,512]{1,0:T(8,128)} %param.20) | copy-start | bytes 786436
  369.0 104.4 %copy-start.8 = (f32[128,512]{1,0:T(8,128)S(1)}, f32[128,512]{1,0:T(8,128)}, u32[]{:S(2)}) copy-start(f32[128,512]{1,0:T(8,128)} %param.21) | copy-start | bytes 786436
  386.0 89.3 %copy-start.2 = (bf16[1536,512]{1,0:T(8,128)(2,1)S(1)}, bf16[1536,512]{1,0:T(8,128)(2,1)}, u32[]{:S(2)}) copy-start(bf16[1536,512]{1,0:T(8,128)(2,1)} %all-gather.3.cloned.1.call-done) | copy-start | bytes 4718596
  464.7 11.7 %copy-start.5 = (f32[128,512]{1,0:T(8,128)}, f32[128,512]{1,0:T(8,128)S(1)}, u32[]{:S(2)}) copy-start(f32[128,512]{1,0:T(8,128)S(1)} %sub.9) | copy-start | bytes 786436
  464.7 11.7 %copy-start.3 = (bf16[1536,512]{1,0:T(8,128)(2,1)S(1)}, bf16[1536,512]{1,0:T(8,128)(2,1)}, u32[]{:S(2)}) copy-start(bf16[1536,512]{1,0:T(8,128)(2,1)} %all-gather.5.cloned.1.call-done) | copy-start | bytes 4718596
  466.2 11.4 %copy-start.6 = (bf16[128,512]{1,0:T(8,128)(2,1)}, bf16[128,512]{1,0:T(8,128)(2,1)S(1)}, u32[]{:S(2)}) copy-start(bf16[128,512]{1,0:T(8,128)(2,1)S(1)} %fusion.4) | copy-start | bytes 393220
Sparse Core Ops, SparseCore 0:
  13.0 213.0 all-reduce.6
  255.5 36.9 reduce-scatter.2
  294.7 19.6 all-gather.2
  323.8 37.9 reduce-scatter.4
  364.3 19.6 all-gather.4
  388.1 75.5 all-reduce.4
where the time goes:
time: 486 us; the launch traced here: 484 us
  waiting for transfers between devices  329 us (68%)
  local copies, waits for them, and re-layouts  48.9 us (10%)
  matrix products  45 us (9%)
  other arithmetic  40.1 us (8%)
  between operations  14.3 us (3%)
  blocking collectives  7.15 us (1%)
    psum x1, waiting for transfers between devices, spread_2(): return lax.psum(kept, axis)  191 us
    psum x1, waiting for transfers between devices, row_sums(): return lax.psum(pieces_in, 'row')  77.7 us
    reduce_scatter x2, waiting for transfers between devices, finish(): lax.psum_scatter(partial_value, 'col', scatter_dimension=0, tiled=True)  44.8 us
    dot_general x2, matrix products, partial_product(): jnp.dot(row_slab, spread.reshape(col_blocks * BS, W), preferred_element_t...  21.2 us
    gather x2, local copies, waits for them, and re-layouts, partial_product(): jnp.take(slab_blocks, own_rows, axis=0)  19.1 us
    select_n x3, other arithmetic, partial_product(): jnp.take(slab_blocks, own_rows, axis=0)  16.8 us
    all_gather x2, waiting for transfers between devices, finish(): return lax.all_gather(share_out, 'col', axis=0, tiled=True)  14.9 us
    another operation x3, other arithmetic, partial_product(): received = jnp.stack(pieces).reshape(fanout * PAD, BS * W)  11.9 us
  transfers between devices with their start and end apart: 6, of which 5 were waited for; matrix products, arithmetic and copies ran while one was open for 18% of the time, Pallas kernels for 0%

commit v1 on v0

--- a/solution.py
+++ b/solution.py
@@ -11,7 +11,7 @@
 
 def spread_2(value, axis, source):
     kept = jnp.where(lax.axis_index(axis) == source, value, 0).astype(value.dtype)
-    return lax.psum(kept, axis)
+    return jnp.sum(lax.all_gather(kept, axis), axis=0)
 
 
 def contract_rows(former, latter):

time: 486 us -> 952 us (1.96)
  waiting for transfers between devices: 329 us -> 759 us
  other arithmetic: 40.1 us -> 73.1 us
    all_gather x0 -> x4, waiting for transfers between devices: none -> 609 us  [spread_2(): return jnp.sum(lax.all_gather(kept, axis), axis=0)]
    psum x1 -> x0, waiting for transfers between devices: 191 us -> none  [spread_2(): return lax.psum(kept, axis)]
    reduce_sum x0 -> x4, other arithmetic: none -> 31.9 us  [spread_2(): return jnp.sum(lax.all_gather(kept, axis), axis=0)]
    reduce_scatter x2, waiting for transfers between devices: 44.8 us -> 56 us  [finish(): lax.psum_scatter(partial_value, 'col', scatter_dimension=0, tiled=True)]
  transfers between devices with their start and end apart: 6 -> 9, of which waited for: 5 -> 8; matrix products, arithmetic and copies ran while one was open for 18% -> 16% of each run, Pallas kernels for 0% -> 0%
where the time goes in v1:
time: 952 us; the launch traced here: 950 us
  waiting for transfers between devices  759 us (80%)
  other arithmetic  73.1 us (8%)
  local copies, waits for them, and re-layouts  49.5 us (5%)
  matrix products  47 us (5%)
  between operations  14 us (1%)
    all_gather x4, waiting for transfers between devices, spread_2(): return jnp.sum(lax.all_gather(kept, axis), axis=0)  609 us
    psum x1, waiting for transfers between devices, row_sums(): return lax.psum(pieces_in, 'row')  77.8 us
    reduce_scatter x2, waiting for transfers between devices, finish(): lax.psum_scatter(partial_value, 'col', scatter_dimension=0, tiled=True)  56 us
    reduce_sum x4, other arithmetic, spread_2(): return jnp.sum(lax.all_gather(kept, axis), axis=0)  31.9 us
    dot_general x2, matrix products, partial_product(): jnp.dot(row_slab, spread.reshape(col_blocks * BS, W), preferred_element_t...  21.4 us
    gather x2, local copies, waits for them, and re-layouts, partial_product(): jnp.take(slab_blocks, own_rows, axis=0)  19.1 us
  transfers between devices with their start and end apart: 9, of which 8 were waited for; matrix products, arithmetic and copies ran while one was open for 16% of the time, Pallas kernels for 0%

profile of v1, /device:TPU:0, one launch (start us, length us, event | category | flops | bytes accessed | tf_op | source)
XLA Modules:
  0.0 950.2 jit_solution(14562580066250098571)
XLA Ops:
  15.4 9.8 %gather_fusion = bf16[12,128,3072]{2,1,0:T(8,128)(2,1)} fusion(bf16[12,128,3072]{2,1,0:T(8,128)(2,1)} %bitcast.59, s32[1024]{0:T(1024)S(1)} %pad_clamp_fusion.1), kind=kCustom, calls=%fused_computation.clone | custom fusion | bytes 18874416 | tf_op jit(solution)/shard_map/jit(_take)/gather | solution.py:49
  28.8 8.3 broadcast_select_fusion.1
  37.0 152.6 %all-gather.17.cloned.1.call-done = bf16[12288,512]{1,0:T(8,128)(2,1)} async-done(((bf16[1536,512]{1,0:T(8,128)(2,1)}), bf16[12288,512]{1,0:T(8,128)(2,1)}) %all-gather.17.cloned.1.call-update) | async-done | bytes 12582928 | tf_op jit(solution)/shard_map/all_gather | solution.py:14
  189.7 8.0 reduce_sum.49
  197.6 169.1 %all-gather.15.cloned.1.call-done = bf16[12288,512]{1,0:T(8,128)(2,1)} async-done(((bf16[1536,512]{1,0:T(8,128)(2,1)}), bf16[12288,512]{1,0:T(8,128)(2,1)}) %all-gather.15.cloned.1.call-update) | async-done | bytes 12582928 | tf_op jit(solution)/shard_map/all_gather | solution.py:14
  366.7 8.0 reduce_sum.48
  379.1 5.1 reshape.70
  384.3 4.6 convolution_convert_fusion.1
  388.9 5.2 reshape.71
  394.0 10.8 %fusion.53 = f32[1536,512]{1,0:T(8,128)} fusion(bf16[1536,3072]{1,0:T(8,128)(2,1)} %bitcast.66, bf16[3072,512]{1,0:T(8,128)(2,1)} %reshape.71), kind=kOutput, calls=%fused_computation.96 | convolution fusion | flops 4831838208 | bytes 15728640 | tf_op jit(solution)/shard_map/dot_general | solution.py:69
  405.7 9.3 gather_fusion.1
  416.4 8.2 broadcast_select_fusion
  424.7 118.6 %all-gather.19.cloned.1.call-done = bf16[12288,512]{1,0:T(8,128)(2,1)} async-done(((bf16[1536,512]{1,0:T(8,128)(2,1)}), bf16[12288,512]{1,0:T(8,128)(2,1)}) %all-gather.19.cloned.1.call-update) | async-done | bytes 12582928 | tf_op jit(solution)/shard_map/all_gather | solution.py:14
  543.3 8.0 reduce_sum.50
  551.2 168.4 %all-gather.21.cloned.1.call-done = bf16[12288,512]{1,0:T(8,128)(2,1)} async-done(((bf16[1536,512]{1,0:T(8,128)(2,1)}), bf16[12288,512]{1,0:T(8,128)(2,1)}) %all-gather.21.cloned.1.call-update) | async-done | bytes 12582928 | tf_op jit(solution)/shard_map/all_gather | solution.py:14
  719.6 8.0 reduce_sum.51
  727.6 30.5 %reduce-scatter.3.cloned.1.call-done = f32[384,512]{1,0:T(8,128)} async-done(((f32[1536,512]{1,0:T(8,128)}), f32[384,512]{1,0:T(8,128)}) %reduce-scatter.3.cloned.1.call-update) | async-done | bytes 786448 | tf_op jit(solution)/shard_map/reduce_scatter | solution.py:75
  764.1 5.2 reshape.73
  773.8 5.2 reshape.74
  779.0 10.7 %fusion.54 = f32[1536,512]{1,0:T(8,128)} fusion(bf16[1536,3072]{1,0:T(8,128)(2,1)} %bitcast.65, bf16[3072,512]{1,0:T(8,128)(2,1)} %reshape.74), kind=kOutput, calls=%fused_computation.97 | convolution fusion | flops 4831838208 | bytes 15728640 | tf_op jit(solution)/shard_map/dot_general | solution.py:69
  802.2 25.5 %reduce-scatter.5.cloned.1.call-done = f32[384,512]{1,0:T(8,128)} async-done(((f32[1536,512]{1,0:T(8,128)}), f32[384,512]{1,0:T(8,128)}) %reduce-scatter.5.cloned.1.call-update) | async-done | bytes 786448 | tf_op jit(solution)/shard_map/reduce_scatter | solution.py:75
  835.0 14.9 %all-gather.13.cloned.1.call-done = bf16[1536,512]{1,0:T(8,128)(2,1)} async-done(((bf16[384,512]{1,0:T(8,128)(2,1)}), bf16[1536,512]{1,0:T(8,128)(2,1)}) %all-gather.13.cloned.1.call-update) | async-done | bytes 1572880 | tf_op jit(solution)/shard_map/all_gather | solution.py:80
  852.0 77.8 %all-reduce.3.cloned.1.call-done = (f32[128,512]{1,0:T(8,128)}, f32[128,512]{1,0:T(8,128)}, f32[128,512]{1,0:T(8,128)}) async-done(((f32[128,512]{1,0:T(8,128)}, f32[128,512]{1,0:T(8,128)}, f32[128,512]{1,0:T(8,128)}), (f32[128,512]{1,0:T(8,128)}, f32[128,512]{1,0:T(8,128)}, f32[128,512]{1,0:T(8,128)})) %all-reduce.3.cloned.1.call-update) | async-done | bytes 786448 | tf_op jit(solution)/shard_map/psum | solution.py:83
  932.3 7.2 all_gather.43
  (82 shorter events, 57.4 us)
Async XLA Ops:
  7.2 820.5 %copy-start = (bf16[512,512]{1,0:T(8,128)(2,1)S(1)}, bf16[512,512]{1,0:T(8,128)(2,1)}, u32[]{:S(2)}) copy-start(bf16[512,512]{1,0:T(8,128)(2,1)} %param.19) | copy-start | bytes 1572868
  7.2 182.5 %all-gather.17.cloned.1.call-start = ((), (), s32[]{:S(2)}) async-start(), calls=%async_computation.7 | async-start | bytes 14155776 | tf_op jit(solution)/shard_map/all_gather | solution.py:14
  7.2 4.2 copy-start.1
  10.7 356.1 %all-gather.15.cloned.1.call-start = ((), (), s32[]{:S(2)}) async-start(), calls=%async_computation.6 | async-start | bytes 14155776 | tf_op jit(solution)/shard_map/all_gather | solution.py:14
  11.4 531.8 %all-gather.19.cloned.1.call-start = ((), (), s32[]{:S(2)}) async-start(), calls=%async_computation.8 | async-start | bytes 14155776 | tf_op jit(solution)/shard_map/all_gather | solution.py:14
  13.4 706.3 %all-gather.21.cloned.1.call-start = ((), (), s32[]{:S(2)}) async-start(), calls=%async_computation.9 | async-start | bytes 14155776 | tf_op jit(solution)/shard_map/all_gather | solution.py:14
  13.9 744.2 %reduce-scatter.3.cloned.1.call-start = ((), (), s32[]{:S(2)}) async-start(), calls=%async_computation.2 | async-start | bytes 3932160 | tf_op jit(solution)/shard_map/reduce_scatter | solution.py:75
  15.4 9.8 %copy-start.8 = (s32[8]{0:T(128)S(1)}, s32[8]{0:T(128)}, u32[]{:S(2)}) copy-start(s32[8]{0:T(128)} %param.17) | copy-start | bytes 100
  15.4 9.8 %copy-start.9 = (s32[8]{0:T(128)S(1)}, s32[8]{0:T(128)}, u32[]{:S(2)}) copy-start(s32[8]{0:T(128)} %param.14) | copy-start | bytes 100
  404.8 387.1 %all-gather.11.cloned.1.call-start = ((), (), s32[]{:S(2)}) async-start(), calls=%async_computation.3 | async-start | bytes 1966080 | tf_op jit(solution)/shard_map/all_gather | solution.py:80
  760.2 67.6 %reduce-scatter.5.cloned.1.call-start = ((), (), s32[]{:S(2)}) async-start(), calls=%async_computation.4 | async-start | bytes 3932160 | tf_op jit(solution)/shard_map/reduce_scatter | solution.py:75
  789.7 60.2 %all-gather.13.cloned.1.call-start = ((), (), s32[]{:S(2)}) async-start(), calls=%async_computation.5 | async-start | bytes 1966080 | tf_op jit(solution)/shard_map/all_gather | solution.py:80
  830.1 99.7 %all-reduce.3.cloned.1.call-start = ((), (), s32[]{:S(2)}) async-start(), calls=%async_computation.10 | async-start | bytes 1572864 | tf_op jit(solution)/shard_map/psum | solution.py:83
  832.3 97.6 %copy-start.6 = (f32[128,512]{1,0:T(8,128)S(1)}, f32[128,512]{1,0:T(8,128)}, u32[]{:S(2)}) copy-start(f32[128,512]{1,0:T(8,128)} %param.20) | copy-start | bytes 786436
  835.0 104.5 %copy-start.7 = (f32[128,512]{1,0:T(8,128)S(1)}, f32[128,512]{1,0:T(8,128)}, u32[]{:S(2)}) copy-start(f32[128,512]{1,0:T(8,128)} %param.21) | copy-start | bytes 786436
  852.0 89.4 %copy-start.2 = (bf16[1536,512]{1,0:T(8,128)(2,1)S(1)}, bf16[1536,512]{1,0:T(8,128)(2,1)}, u32[]{:S(2)}) copy-start(bf16[1536,512]{1,0:T(8,128)(2,1)} %all-gather.11.cloned.1.call-done) | copy-start | bytes 4718596
  930.8 11.7 %copy-start.4 = (f32[128,512]{1,0:T(8,128)}, f32[128,512]{1,0:T(8,128)S(1)}, u32[]{:S(2)}) copy-start(f32[128,512]{1,0:T(8,128)S(1)} %sub.9) | copy-start | bytes 786436
  930.9 11.7 %copy-start.3 = (bf16[1536,512]{1,0:T(8,128)(2,1)S(1)}, bf16[1536,512]{1,0:T(8,128)(2,1)}, u32[]{:S(2)}) copy-start(bf16[1536,512]{1,0:T(8,128)(2,1)} %all-gather.13.cloned.1.call-done) | copy-start | bytes 4718596
  932.3 11.4 %copy-start.5 = (bf16[128,512]{1,0:T(8,128)(2,1)}, bf16[128,512]{1,0:T(8,128)(2,1)S(1)}, u32[]{:S(2)}) copy-start(bf16[128,512]{1,0:T(8,128)(2,1)S(1)} %fusion.4) | copy-start | bytes 393220
Sparse Core Ops, SparseCore 0:
  10.8 178.8 all-gather.16
  192.4 174.2 all-gather.14
  368.9 174.2 all-gather.18
  545.3 174.2 all-gather.20
  722.0 36.0 reduce-scatter.2
  760.3 19.6 all-gather.10
  789.8 37.8 reduce-scatter.4
  830.2 19.6 all-gather.12
  854.2 75.5 all-reduce.2
